TPU v7x, 32 devices: a whole 2x2x4 slice. The times are simulated.
32 devices in a mesh: groups: 2 (over x), tile: 16 (over z, y, core).
Axes of the slice: x: 2, y: 2, z: 4, core: 2. Of those that a mesh axis runs over, the one named last changes fastest.
Arguments:
- hidden: bfloat16 [12288, 1152], P(('groups', 'tile')), parts along dimension 0, may hold values from -40 to 40
- keep_mask: int32 [12288], P(('groups', 'tile')), parts along dimension 0, may hold values 0 or 1
- kept_embed: bfloat16 [1152], replicated, may hold values from -6 to 6
- time_mod: bfloat16 [50, 6, 1152], replicated, may hold values from -3 to 3
- timestep: int32 [2], P('groups'), parts along dimension 0, may hold values from 0 to 49
- qkv_weight: bfloat16 [1152, 3456], replicated, may hold values from -0.1875 to 0.1875
- proj_weight: bfloat16 [1152, 1152], replicated, may hold values from -0.1875 to 0.1875
- norm_gain: bfloat16 [1152], replicated, may hold values from 0.099609375 to 1.8984375
- in_weight: bfloat16 [1152, 5760], P('tile'), may hold values from -0.1875 to 0.1875
- in_bias: bfloat16 [5760], replicated, may hold values from -3 to 3
- conv_weight: bfloat16 [3, 3, 5760], replicated, may hold values from -2 to 2
- conv_bias: bfloat16 [5760], replicated, may hold values from -3 to 3
- out_weight: bfloat16 [2880, 1152], P(None, 'tile'), may hold values from -0.109375 to 0.109375
Outputs:
- output: bfloat16 [12288, 1152], P(('groups', 'tile')), parts along dimension 0
There are 2 independent parts, one for each index of `groups`. A program takes and returns all parts, laid end to end along the dimension named above; an argument that names none is the same for every part. Nothing has to cross between parts.
All inputs are finite; a program needn't handle non-finite values. No bound on the sum of `keep_mask` on one device may be relied on, other than what follows from the above.
Results may differ from a plain program's by a relative error of at most 0.0015.
The roundings to bfloat16 on the way count: a program that leaves them out, or rounds other values in their place, can miss the bound.
Values may be sent and summed in bfloat16 or wider, within the bound.
A program may use at most 192 MiB of HBM per device.

v0:
```python
import jax
import jax.numpy as jnp
from jax import lax
from jax.sharding import PartitionSpec as P

D = 1152
HEADS = 36
HEAD_DIM = 32
FF = 2880
CANVAS_W = 128


def padded_2(cells, sides, width):
    for axis, dim in sides:
        count = lax.axis_size(axis)
        ends = count - 1
        head = lax.slice_in_dim(cells, 0, width, axis=dim)
        tail = lax.slice_in_dim(cells, cells.shape[dim] - width, cells.shape[dim], axis=dim)
        cells = jnp.concatenate(
            [
                lax.ppermute(tail, axis, [(i, (i + 1) % count) for i in range(ends)]),
                cells,
                lax.ppermute(head, axis, [((i + 1) % count, i) for i in range(ends)]),
            ],
            axis=dim,
        )
    return cells


def modulated_norm(stream, shift, scale):
    factor = lax.rsqrt(jnp.mean(stream * stream, axis=-1, keepdims=True) + 1e-06)
    return stream * factor * (1.0 + scale) + shift


def convolve(window, conv_weight, conv_bias, count):
    width = window.shape[1] - 2
    total = jnp.zeros((count, width, window.shape[2]), jnp.float32) + conv_bias.astype(jnp.float32)
    for row_off in range(3):
        for col_off in range(3):
            total = total + window[row_off : row_off + count, col_off : col_off + width, :].astype(
                jnp.float32
            ) * conv_weight[row_off, col_off].astype(jnp.float32)
    return total


def row_folder(source, piece):
    return jnp.dot(source, piece, preferred_element_type=jnp.float32)


def local(
    hidden,
    keep_mask,
    kept_embed,
    time_mod,
    timestep,
    qkv_weight,
    proj_weight,
    norm_gain,
    in_weight,
    in_bias,
    conv_weight,
    conv_bias,
    out_weight,
):
    modulation = lax.dynamic_index_in_dim(time_mod, timestep[0], 0, keepdims=False).astype(
        jnp.float32
    )
    tokens = hidden.shape[0]
    rows = tokens // CANVAS_W
    stream = (
        hidden.astype(jnp.float32)
        + keep_mask.astype(jnp.float32)[:, None] * kept_embed.astype(jnp.float32)[None, :]
    )
    normed_in = modulated_norm(stream, modulation[0], modulation[1]).astype(jnp.bfloat16)
    mixed_qkv = jnp.dot(normed_in, qkv_weight, preferred_element_type=jnp.float32)
    query = jax.nn.relu(mixed_qkv[:, :D]).astype(jnp.bfloat16).reshape(tokens, HEADS, HEAD_DIM)
    key_rows = (
        jax.nn.relu(mixed_qkv[:, D : 2 * D]).astype(jnp.bfloat16).reshape(tokens, HEADS, HEAD_DIM)
    )
    values = mixed_qkv[:, 2 * D :].astype(jnp.bfloat16).reshape(tokens, HEADS, HEAD_DIM)
    local_state = jnp.einsum("thd,the->hde", key_rows, values, preferred_element_type=jnp.float32)
    state = lax.psum(local_state, "tile")
    attended = jnp.einsum(
        "thd,hde->the", query.astype(jnp.float32), state, precision=lax.Precision.HIGHEST
    ).reshape(tokens, D)
    factor = lax.rsqrt(jnp.mean(attended * attended, axis=-1, keepdims=True) + 1e-06)
    normed_attn = (attended * factor * norm_gain.astype(jnp.float32)).astype(jnp.bfloat16)
    after_attn = stream + modulation[2] * jnp.dot(
        normed_attn, proj_weight, preferred_element_type=jnp.float32
    )
    normed_ffn = modulated_norm(after_attn, modulation[3], modulation[4]).astype(jnp.bfloat16)
    before = row_folder(normed_ffn, lax.all_gather(in_weight, "tile", axis=0, tiled=True))
    inner = (
        jax.nn.silu(before + in_bias.astype(jnp.float32))
        .astype(jnp.bfloat16)
        .reshape(rows, CANVAS_W, 2 * FF)
    )
    framed = padded_2(inner, (("tile", 0),), 1)
    padded = jnp.pad(framed, ((0, 0), (1, 1), (0, 0)))
    conv = convolve(padded, conv_weight, conv_bias, rows)
    gated = (conv[..., :FF] * jax.nn.silu(conv[..., FF:])).astype(jnp.bfloat16).reshape(tokens, FF)
    projected = jnp.dot(
        gated,
        lax.all_gather(out_weight, "tile", axis=1, tiled=True),
        preferred_element_type=jnp.float32,
    )
    return (after_attn + modulation[5] * projected).astype(jnp.bfloat16)


def solution(mesh):
    in_specs = (
        P(("groups", "tile"), None),
        P(("groups", "tile")),
        P(),
        P(),
        P("groups"),
        P(),
        P(),
        P(),
        P("tile", None),
        P(),
        P(),
        P(),
        P(None, "tile"),
    )
    out_specs = P(("groups", "tile"), None)
    return jax.shard_map(local, mesh=mesh, in_specs=in_specs, out_specs=out_specs, check_vma=False)
```

profile of v0, /device:TPU:0, one launch (start us, length us, event | category | flops | bytes accessed | tf_op | source)
XLA Modules:
  0.0 325.5 jit_solution(18351720821955758159)
XLA Ops:
  7.3 0.9 dynamic-slice_convert_fusion
  10.3 1.6 multiply_reduce_fusion.1
  11.9 7.5 %fusion.15 = bf16[384,3456]{1,0:T(8,128)(2,1)S(1)} fusion(bf16[1152,3456]{1,0:T(8,128)(2,1)} %param.18, bf16[384,1152]{1,0:T(8,128)(2,1)} %param.13, f32[1152]{0:T(1024)S(1)} %get-tuple-element.17, f32[1152]{0:T(1024)S(1)} %get-tuple-element.18, f32[384]{0:T(512)S(1)} %add_rsqrt_fusion.2, f32[1152]{0:T(1024)S(1)} %convert_element_type.97, ...), kind=kOutput, calls=%fused_computation.36 | convolution fusion | flops 3060744192 | bytes 11518464 | tf_op jit(solution)/shard_map/dot_general | solution.py:75
  19.4 1.6 fusion.10
  21.0 1.7 copy.15
  22.8 2.2 copy.16
  25.0 2.4 fusion.26
  27.5 0.7 all-gather.3.cloned.1.call-update
  29.0 1.8 copy.17
  31.4 1.3 convert_element_type.106
  32.7 89.1 %all-reduce.3.cloned.1.call-done = f32[36,32,32]{1,2,0:T(8,128)} async-done(((f32[36,32,32]{1,2,0:T(8,128)}), f32[36,32,32]{1,2,0:T(8,128)}) %all-reduce.3.cloned.1.call-update) | async-done | bytes 147472 | tf_op jit(solution)/shard_map/psum | solution.py:82
  121.8 2.1 fusion.14
  124.2 2.9 multiply_reduce_fusion
  127.1 101.0 %all-gather.3.cloned.1.call-done = bf16[1152,5760]{1,0:T(8,128)(2,1)} async-done(((bf16[72,5760]{1,0:T(8,128)(2,1)}), bf16[1152,5760]{1,0:T(8,128)(2,1)}) %all-gather.3.cloned.1.call-update) | async-done | bytes 13271056 | tf_op jit(solution)/shard_map/all_gather | solution.py:92
  228.1 11.6 %multiply_convert_fusion = bf16[384,5760]{1,0:T(8,128)(2,1)S(1)} fusion(bf16[1152,5760]{1,0:T(8,128)(2,1)} %all-gather.3.cloned.1.call-done, f32[5760]{0:T(1024)S(1)} %copy-done.5, f32[384,1152]{1,0:T(8,128)} %get-tuple-element.28, f32[1152]{0:T(1024)S(1)} %copy-done.10, f32[1152]{0:T(1024)S(1)} %copy-done.11, f32[384]{0:T(512)S(1)} %add_rsqrt_fusion), kind=kOutput, calls=%fused_computation.7 | convolution fusion | flops 5111119872 | bytes 19497984 | tf_op jit(solution)/shard_map/dot_general | solution.py:47
  239.9 2.3 collective-permute-start
  242.2 1.5 collective-permute-start.1
  244.3 1.1 convert_reduce_fusion.8
  245.4 1.9 collective-permute-done.1
  247.4 3.0 fusion.5
  250.4 10.6 %multiply_add_fusion = f32[3,128,5760]{2,1,0:T(8,128)S(1)} fusion(bf16[3,128,5760]{2,1,0:T(8,128)(2,1)S(1)} %bitcast.35, bf16[5,130,5760]{2,1,0:T(8,128)(2,1)S(1)} %fusion.5, bf16[1,128,5760]{2,1,0:T(8,128)(2,1)} %copy-done.2, bf16[1,128,5760]{2,1,0:T(8,128)(2,1)S(1)} %collective-permute-done, f32[5760]{0:T(1024)} %get-tuple-element.12, ...), kind=kLoop, calls=%fused_computation.6 | loop fusion | flops 64143360 | bytes 42992640 | tf_op jit(solution)/shard_map/add | solution.py:40
  261.0 2.8 fusion.6
  263.8 46.9 %all-gather.5.cloned.1.call-done = bf16[2880,1152]{0,1:T(8,128)(2,1)} async-done(((bf16[2880,72]{0,1:T(8,128)(2,1)}), bf16[2880,1152]{0,1:T(8,128)(2,1)}) %all-gather.5.cloned.1.call-update) | async-done | bytes 6635536 | tf_op jit(solution)/shard_map/all_gather | solution.py:104
  310.7 8.4 %fusion.9 = bf16[384,1152]{1,0:T(8,128)(2,1)} fusion(f32[384,1152]{1,0:T(8,128)} %get-tuple-element.28, bf16[384,2880]{1,0:T(8,128)(2,1)} %bitcast.39, bf16[2880,1152]{0,1:T(8,128)(2,1)} %all-gather.5.cloned.1.call-done, f32[1152]{0:T(1024)S(1)} %copy-done.9), kind=kOutput, calls=%fused_computation.18 | convolution fusion | flops 2549366784 | bytes 11506176 | tf_op jit(solution)/shard_map/dot_general | solution.py:102
  (42 shorter events, 4.6 us)
Async XLA Ops:
  6.5 117.6 %copy-start = (bf16[1152,1152]{1,0:T(8,128)(2,1)S(1)}, bf16[1152,1152]{1,0:T(8,128)(2,1)}, u32[]{:S(2)}) copy-start(bf16[1152,1152]{1,0:T(8,128)(2,1)} %param.19) | copy-start | bytes 7962628
  6.5 115.3 %all-reduce.3.cloned.1.call-start = ((), (), s32[]{:S(2)}) async-start(), calls=%async_computation | async-start | bytes 1179648 | tf_op jit(solution)/shard_map/psum | solution.py:82
  10.3 9.1 %copy-start.7 = (f32[384]{0:T(512)}, f32[384]{0:T(512)S(1)}, u32[]{:S(2)}) copy-start(f32[384]{0:T(512)S(1)} %convert_element_type.96) | copy-start | bytes 4612
  27.5 200.6 %all-gather.3.cloned.1.call-start = ((), (), s32[]{:S(2)}) async-start(), calls=%async_computation.1 | async-start | bytes 14100480 | tf_op jit(solution)/shard_map/all_gather | solution.py:92
  28.2 282.4 %all-gather.5.cloned.1.call-start = ((), (), s32[]{:S(2)}) async-start(), calls=%async_computation.2 | async-start | bytes 7206912 | tf_op jit(solution)/shard_map/all_gather | solution.py:104
  121.8 2.4 copy-start.3
  121.8 2.4 copy-start.8
  121.8 2.4 copy-start.12
  124.1 103.9 %copy-start.5 = (f32[5760]{0:T(1024)S(1)}, f32[5760]{0:T(1024)}, u32[]{:S(2)}) copy-start(f32[5760]{0:T(1024)} %convert_element_type.106) | copy-start | bytes 69124
  124.2 103.9 %copy-start.10 = (f32[1152]{0:T(1024)S(1)}, f32[1152]{0:T(1024)}, u32[]{:S(2)}) copy-start(f32[1152]{0:T(1024)} %get-tuple-element.15) | copy-start | bytes 13828
  124.2 103.9 %copy-start.11 = (f32[1152]{0:T(1024)S(1)}, f32[1152]{0:T(1024)}, u32[]{:S(2)}) copy-start(f32[1152]{0:T(1024)} %get-tuple-element.16) | copy-start | bytes 13828
  239.7 4.0 %copy-start.6 = (bf16[5760]{0:T(1024)(128)(2,1)S(1)}, bf16[5760]{0:T(1024)(128)(2,1)}, u32[]{:S(2)}) copy-start(bf16[5760]{0:T(1024)(128)(2,1)} %param.24) | copy-start | bytes 34564
  239.7 4.6 %copy-start.4 = (bf16[3,3,5760]{2,1,0:T(4,128)(2,1)S(1)}, bf16[3,3,5760]{2,1,0:T(4,128)(2,1)}, u32[]{:S(2)}) copy-start(bf16[3,3,5760]{2,1,0:T(4,128)(2,1)} %param.23) | copy-start | bytes 311044
  239.9 5.5 %collective-permute-start = (bf16[1,128,5760]{2,1,0:T(8,128)(2,1)S(1)}, bf16[1,128,5760]{2,1,0:T(8,128)(2,1)S(1)}, u32[]{:S(2)}, u32[]{:S(2)}) collective-permute-start(bf16[1,128,5760]{2,1,0:T(8,128)(2,1)S(1)} %get-tuple-element.20), channel_id=1, source_target_pairs={{0,1},{1,2},{2,3},{3,4},{4,5},{5,6},{6,7},{7,8},{8,9},{9,10},{10,1... | collective-permute-start | bytes 4423688 | tf_op jit(solution)/shard_map/ppermute | solution.py:21
  242.2 5.2 %collective-permute-start.1 = (bf16[1,128,5760]{2,1,0:T(8,128)(2,1)S(1)}, bf16[1,128,5760]{2,1,0:T(8,128)(2,1)S(1)}, u32[]{:S(2)}, u32[]{:S(2)}) collective-permute-start(bf16[1,128,5760]{2,1,0:T(8,128)(2,1)S(1)} %get-tuple-element.21), channel_id=1, source_target_pairs={{1,0},{2,1},{3,2},{4,3},{5,4},{6,5},{7,6},{8,7},{9,8},{10,9},{11,1... | collective-permute-start | bytes 4423688 | tf_op jit(solution)/shard_map/ppermute | solution.py:23
  247.4 3.0 copy-start.2
  261.0 49.7 %copy-start.9 = (f32[1152]{0:T(1024)S(1)}, f32[1152]{0:T(1024)}, u32[]{:S(2)}) copy-start(f32[1152]{0:T(1024)} %get-tuple-element.14) | copy-start | bytes 13828
  310.7 8.4 %copy-start.1 = (bf16[1152,1152]{1,0:T(8,128)(2,1)S(1)}, bf16[1152,1152]{1,0:T(8,128)(2,1)}, u32[]{:S(2)}) copy-start(bf16[1152,1152]{1,0:T(8,128)(2,1)} %param.19) | copy-start | bytes 7962628
Sparse Core Ops, SparseCore 0:
  27.6 94.1 all-reduce.2
  124.0 104.0 all-gather.2
  230.2 80.3 all-gather.4
where the time goes:
time: 326 us
  waiting for transfers between devices  240 us (74%)
  matrix products  34.8 us (11%)
  other arithmetic  26.6 us (8%)
  between operations  14.1 us (4%)
  local copies, waits for them, and re-layouts  5.99 us (2%)
  starting transfers between devices  3.81 us (1%)
    all_gather x1, waiting for transfers between devices, local(): lax.all_gather(in_weight, 'tile', axis=0, tiled=True)  101 us
    psum x1, waiting for transfers between devices, local(): state = lax.psum(local_state, 'tile')  89.1 us
    all_gather x1, waiting for transfers between devices, local(): lax.all_gather(out_weight, 'tile', axis=1, tiled=True)  46.9 us
    dot_general x1, matrix products, row_folder(): return jnp.dot(source, piece, preferred_element_type=jnp.float32)  11.6 us
    add x1, other arithmetic, convolve(): total + window[row_off:row_off + count, col_off:col_off + width, :].astyp...  10.6 us
    dot_general x1, matrix products, local(): jnp.dot(gated, lax.all_gather(out_weight, 'tile', axis=1, tiled=True), pr...  8.36 us
    dot_general x1, matrix products, local(): jnp.dot(normed_in, qkv_weight, preferred_element_type=jnp.float32)  7.45 us
  transfers between devices with their start and end apart: 5, of which 4 were waited for; matrix products, arithmetic and copies ran while one was open for 12% of the time, Pallas kernels for 0%

commit v1 on v0

--- a/solution.py
+++ b/solution.py
@@ -2,6 +2,7 @@
 import jax.numpy as jnp
 from jax import lax
 from jax.sharding import PartitionSpec as P
+from jax.lax import all_gather
 
 D = 1152
 HEADS = 36
@@ -79,7 +80,12 @@
     )
     values = mixed_qkv[:, 2 * D :].astype(jnp.bfloat16).reshape(tokens, HEADS, HEAD_DIM)
     local_state = jnp.einsum("thd,the->hde", key_rows, values, preferred_element_type=jnp.float32)
-    state = lax.psum(local_state, "tile")
+
+    def pack_halves(dev_axis, my_data):
+        w1 = all_gather(my_data, dev_axis)
+        return jnp.sum(w1, axis=0)
+
+    state = pack_halves("tile", local_state)
     attended = jnp.einsum(
         "thd,hde->the", query.astype(jnp.float32), state, precision=lax.Precision.HIGHEST
     ).reshape(tokens, D)

time: 326 us -> 315 us (0.966)
  waiting for transfers between devices: 240 us -> 223 us
  other arithmetic: 26.6 us -> 32.3 us
    psum x1 -> x0, waiting for transfers between devices: 89.1 us -> none  [local(): state = lax.psum(local_state, 'tile')]
    all_gather x0 -> x1, waiting for transfers between devices: none -> 79.1 us  [pack_halves(): w1 = all_gather(my_data, dev_axis)]
    all_gather x1, waiting for transfers between devices: 101 us -> 94.3 us  [local(): lax.all_gather(in_weight, 'tile', axis=0, tiled=True)]
    reduce_sum x0 -> x1, other arithmetic: none -> 5.74 us  [pack_halves(): return jnp.sum(w1, axis=0)]
  transfers between devices with their start and end apart: 5 -> 5, of which waited for: 4 -> 4; matrix products, arithmetic and copies ran while one was open for 12% -> 14% of each run, Pallas kernels for 0% -> 0%
where the time goes in v1:
time: 315 us
  waiting for transfers between devices  223 us (71%)
  matrix products  34.9 us (11%)
  other arithmetic  32.3 us (10%)
  between operations  14.1 us (4%)
  local copies, waits for them, and re-layouts  5.99 us (2%)
  starting transfers between devices  4.03 us (1%)
    all_gather x1, waiting for transfers between devices, local(): lax.all_gather(in_weight, 'tile', axis=0, tiled=True)  94.3 us
    all_gather x1, waiting for transfers between devices, pack_halves(): w1 = all_gather(my_data, dev_axis)  79.1 us
    all_gather x1, waiting for transfers between devices, local(): lax.all_gather(out_weight, 'tile', axis=1, tiled=True)  46.9 us
    dot_general x1, matrix products, row_folder(): return jnp.dot(source, piece, preferred_element_type=jnp.float32)  11.6 us
    add x1, other arithmetic, convolve(): total + window[row_off:row_off + count, col_off:col_off + width, :].astyp...  10.6 us
    dot_general x1, matrix products, local(): jnp.dot(gated, lax.all_gather(out_weight, 'tile', axis=1, tiled=True), pr...  8.35 us
    dot_general x1, matrix products, local(): jnp.dot(normed_in, qkv_weight, preferred_element_type=jnp.float32)  7.45 us
  transfers between devices with their start and end apart: 5, of which 4 were waited for; matrix products, arithmetic and copies ran while one was open for 14% of the time, Pallas kernels for 0%

profile of v1, /device:TPU:0, one launch (start us, length us, event | category | flops | bytes accessed | tf_op | source)
XLA Modules:
  0.0 314.7 jit_solution(8181897770527916017)
XLA Ops:
  7.3 0.9 dynamic-slice_convert_fusion
  10.3 1.6 multiply_reduce_fusion.1
  11.9 7.4 %fusion.15 = bf16[384,3456]{1,0:T(8,128)(2,1)S(1)} fusion(bf16[1152,3456]{1,0:T(8,128)(2,1)} %param.18, bf16[384,1152]{1,0:T(8,128)(2,1)} %param.13, f32[1152]{0:T(1024)S(1)} %get-tuple-element.17, f32[1152]{0:T(1024)S(1)} %get-tuple-element.18, f32[384]{0:T(512)S(1)} %add_rsqrt_fusion.2, f32[1152]{0:T(1024)S(1)} %convert_element_type.97, ...), kind=kOutput, calls=%fused_computation.36 | convolution fusion | flops 3060744192 | bytes 11518464 | tf_op jit(solution)/shard_map/dot_general | solution.py:76
  19.4 1.6 fusion.10
  21.0 1.7 copy.20
  22.8 2.2 copy.21
  25.0 2.4 fusion.26
  29.0 1.8 copy.22
  31.4 1.3 convert_element_type.106
  32.7 79.1 %all-gather.9.cloned.1.call-done = f32[576,32,32]{2,1,0:T(8,128)} async-done(((f32[36,32,32]{2,1,0:T(8,128)}), f32[576,32,32]{2,1,0:T(8,128)}) %all-gather.9.cloned.1.call-update) | async-done | bytes 2359312 | tf_op jit(solution)/shard_map/all_gather | solution.py:85
  111.8 5.7 %reduce_sum.37 = f32[36,32,32]{2,1,0:T(8,128)} reduce(f32[16,36,32,32]{3,2,1,0:T(8,128)} %bitcast.37, f32[]{:T(128)} %constant.22.clone.1), dimensions={0}, to_apply=%region_1.2 | reduce | flops 552960 | bytes 2506756 | tf_op jit(solution)/shard_map/reduce_sum | solution.py:86
  117.5 2.1 fusion.14
  120.0 2.8 multiply_reduce_fusion
  122.9 94.3 %all-gather.5.cloned.1.call-done = bf16[1152,5760]{1,0:T(8,128)(2,1)} async-done(((bf16[72,5760]{1,0:T(8,128)(2,1)}), bf16[1152,5760]{1,0:T(8,128)(2,1)}) %all-gather.5.cloned.1.call-update) | async-done | bytes 13271056 | tf_op jit(solution)/shard_map/all_gather | solution.py:98
  217.2 11.6 %multiply_convert_fusion = bf16[384,5760]{1,0:T(8,128)(2,1)S(1)} fusion(bf16[1152,5760]{1,0:T(8,128)(2,1)} %all-gather.5.cloned.1.call-done, f32[5760]{0:T(1024)S(1)} %copy-done.5, f32[384,1152]{1,0:T(8,128)} %get-tuple-element.28, f32[1152]{0:T(1024)S(1)} %copy-done.10, f32[1152]{0:T(1024)S(1)} %copy-done.11, f32[384]{0:T(512)S(1)} %add_rsqrt_fusion), kind=kOutput, calls=%fused_computation.7 | convolution fusion | flops 5111119872 | bytes 19497984 | tf_op jit(solution)/shard_map/dot_general | solution.py:48
  229.1 2.3 collective-permute-start
  231.3 1.5 collective-permute-start.1
  233.5 1.1 convert_reduce_fusion.8
  234.6 1.9 collective-permute-done.1
  236.5 3.0 fusion.5
  239.5 10.6 %multiply_add_fusion = f32[3,128,5760]{2,1,0:T(8,128)S(1)} fusion(bf16[3,128,5760]{2,1,0:T(8,128)(2,1)S(1)} %bitcast.36, bf16[5,130,5760]{2,1,0:T(8,128)(2,1)S(1)} %fusion.5, bf16[1,128,5760]{2,1,0:T(8,128)(2,1)} %copy-done.2, bf16[1,128,5760]{2,1,0:T(8,128)(2,1)S(1)} %collective-permute-done, f32[5760]{0:T(1024)} %get-tuple-element.12, ...), kind=kLoop, calls=%fused_computation.6 | loop fusion | flops 64143360 | bytes 42992640 | tf_op jit(solution)/shard_map/add | solution.py:41
  250.1 2.8 fusion.6
  252.9 46.9 %all-gather.7.cloned.1.call-done = bf16[2880,1152]{0,1:T(8,128)(2,1)} async-done(((bf16[2880,72]{0,1:T(8,128)(2,1)}), bf16[2880,1152]{0,1:T(8,128)(2,1)}) %all-gather.7.cloned.1.call-update) | async-done | bytes 6635536 | tf_op jit(solution)/shard_map/all_gather | solution.py:110
  299.8 8.4 %fusion.9 = bf16[384,1152]{1,0:T(8,128)(2,1)} fusion(f32[384,1152]{1,0:T(8,128)} %get-tuple-element.28, bf16[384,2880]{1,0:T(8,128)(2,1)} %bitcast.41, bf16[2880,1152]{0,1:T(8,128)(2,1)} %all-gather.7.cloned.1.call-done, f32[1152]{0:T(1024)S(1)} %copy-done.9), kind=kOutput, calls=%fused_computation.18 | convolution fusion | flops 2549366784 | bytes 11506176 | tf_op jit(solution)/shard_map/dot_general | solution.py:108
  (43 shorter events, 5.3 us)
Async XLA Ops:
  6.5 113.4 %copy-start = (bf16[1152,1152]{1,0:T(8,128)(2,1)S(1)}, bf16[1152,1152]{1,0:T(8,128)(2,1)}, u32[]{:S(2)}) copy-start(bf16[1152,1152]{1,0:T(8,128)(2,1)} %param.19) | copy-start | bytes 7962628
  6.5 105.2 %all-gather.9.cloned.1.call-start = ((), (), s32[]{:S(2)}) async-start(), calls=%async_computation.2 | async-start | bytes 10027008 | tf_op jit(solution)/shard_map/all_gather | solution.py:85
  10.3 9.1 %copy-start.7 = (f32[384]{0:T(512)}, f32[384]{0:T(512)S(1)}, u32[]{:S(2)}) copy-start(f32[384]{0:T(512)S(1)} %convert_element_type.96) | copy-start | bytes 4612
  27.5 189.7 %all-gather.5.cloned.1.call-start = ((), (), s32[]{:S(2)}) async-start(), calls=%async_computation | async-start | bytes 14100480 | tf_op jit(solution)/shard_map/all_gather | solution.py:98
  28.2 271.5 %all-gather.7.cloned.1.call-start = ((), (), s32[]{:S(2)}) async-start(), calls=%async_computation.1 | async-start | bytes 7206912 | tf_op jit(solution)/shard_map/all_gather | solution.py:110
  117.5 2.5 copy-start.3
  117.5 2.5 copy-start.8
  117.5 2.5 copy-start.12
  119.9 97.2 %copy-start.5 = (f32[5760]{0:T(1024)S(1)}, f32[5760]{0:T(1024)}, u32[]{:S(2)}) copy-start(f32[5760]{0:T(1024)} %convert_element_type.106) | copy-start | bytes 69124
  119.9 97.2 %copy-start.10 = (f32[1152]{0:T(1024)S(1)}, f32[1152]{0:T(1024)}, u32[]{:S(2)}) copy-start(f32[1152]{0:T(1024)} %get-tuple-element.15) | copy-start | bytes 13828
  120.0 97.2 %copy-start.11 = (f32[1152]{0:T(1024)S(1)}, f32[1152]{0:T(1024)}, u32[]{:S(2)}) copy-start(f32[1152]{0:T(1024)} %get-tuple-element.16) | copy-start | bytes 13828
  228.8 4.0 %copy-start.6 = (bf16[5760]{0:T(1024)(128)(2,1)S(1)}, bf16[5760]{0:T(1024)(128)(2,1)}, u32[]{:S(2)}) copy-start(bf16[5760]{0:T(1024)(128)(2,1)} %param.24) | copy-start | bytes 34564
  228.8 4.6 %copy-start.4 = (bf16[3,3,5760]{2,1,0:T(4,128)(2,1)S(1)}, bf16[3,3,5760]{2,1,0:T(4,128)(2,1)}, u32[]{:S(2)}) copy-start(bf16[3,3,5760]{2,1,0:T(4,128)(2,1)} %param.23) | copy-start | bytes 311044
  229.1 5.5 %collective-permute-start = (bf16[1,128,5760]{2,1,0:T(8,128)(2,1)S(1)}, bf16[1,128,5760]{2,1,0:T(8,128)(2,1)S(1)}, u32[]{:S(2)}, u32[]{:S(2)}) collective-permute-start(bf16[1,128,5760]{2,1,0:T(8,128)(2,1)S(1)} %get-tuple-element.20), channel_id=1, source_target_pairs={{0,1},{1,2},{2,3},{3,4},{4,5},{5,6},{6,7},{7,8},{8,9},{9,10},{10,1... | collective-permute-start | bytes 4423688 | tf_op jit(solution)/shard_map/ppermute | solution.py:22
  231.3 5.2 %collective-permute-start.1 = (bf16[1,128,5760]{2,1,0:T(8,128)(2,1)S(1)}, bf16[1,128,5760]{2,1,0:T(8,128)(2,1)S(1)}, u32[]{:S(2)}, u32[]{:S(2)}) collective-permute-start(bf16[1,128,5760]{2,1,0:T(8,128)(2,1)S(1)} %get-tuple-element.21), channel_id=1, source_target_pairs={{1,0},{2,1},{3,2},{4,3},{5,4},{6,5},{7,6},{8,7},{9,8},{10,9},{11,1... | collective-permute-start | bytes 4423688 | tf_op jit(solution)/shard_map/ppermute | solution.py:24
  236.5 3.0 copy-start.2
  250.1 49.7 %copy-start.9 = (f32[1152]{0:T(1024)S(1)}, f32[1152]{0:T(1024)}, u32[]{:S(2)}) copy-start(f32[1152]{0:T(1024)} %get-tuple-element.14) | copy-start | bytes 13828
  299.8 8.4 %copy-start.1 = (bf16[1152,1152]{1,0:T(8,128)(2,1)S(1)}, bf16[1152,1152]{1,0:T(8,128)(2,1)}, u32[]{:S(2)}) copy-start(bf16[1152,1152]{1,0:T(8,128)(2,1)} %param.19) | copy-start | bytes 7962628
Sparse Core Ops, SparseCore 0:
  27.6 84.1 all-gather.8
  113.9 103.2 all-gather.4
  219.3 80.3 all-gather.6
